TPU v7x, 32 devices: a whole 2x2x4 slice. The times are simulated.
32 devices in a mesh: grp: 2 (over x), tmpl: 8 (over z, y), tm: 2 (over core).
Axes of the slice: x: 2, y: 2, z: 4, core: 2. Of those that a mesh axis runs over, the one named last changes fastest.
Arguments:
- spectra: bfloat16 [1024, 4, 8192], P(('grp', 'tm', 'tmpl')), parts along dimension 0, may hold values from -6 to 6
- offsets: int32 [1024, 16], P(('grp', 'tm'), 'tmpl'), parts along dimension 0, may hold values from 0 to 1008
- fractions: float32 [4096], P(('grp', 'tmpl')), parts along dimension 0, may hold values from 0.1 to 0.9
- antenna: float32 [1024, 4], P('grp'), parts along dimension 0, may hold values from -2 to 2, as said below
- starts: int32 [64], P('grp'), parts along dimension 0, may hold values from 0 to 255
- durations: int32 [64], P('grp'), parts along dimension 0, may hold values from 48 to 256
Outputs:
- fstat_map: float32 [32, 32, 4096], P('tm', None, ('grp', 'tmpl')), parts along dimension 2
- loudest: float32 [64, 32], P(('grp', 'tm')), parts along dimension 0
There are 2 independent parts, one for each index of `grp`. A program takes and returns all parts, laid end to end along the dimension named above; each array names one. Nothing has to cross between parts.
Inputs may be any that keep to these rules, and one draw needn't show every extreme that they name: `antenna`: each detector's responses a and b turn once every 48 SFTs with magnitudes that vary from SFT to SFT.
All inputs are finite; a program needn't handle non-finite values.
Results may differ from a plain program's by a relative error of at most 0.0051.
Values may be sent and summed in bfloat16 or wider, within the bound.
A program may use at most 128 MiB of HBM per device.

v0:
```python
import jax
import jax.numpy as jnp
from jax import lax
from jax.sharding import PartitionSpec as P

W = 16


def weigh(windows, antenna):
    values = windows.astype(jnp.float32)
    detector_one = values[:, 0:2]
    detector_two = values[:, 2:4]
    weighted_a = (
        antenna[:, 0][:, None, None, None] * detector_one
        + antenna[:, 1][:, None, None, None] * detector_two
    )
    weighted_b = (
        antenna[:, 2][:, None, None, None] * detector_one
        + antenna[:, 3][:, None, None, None] * detector_two
    )
    return jnp.concatenate([weighted_a, weighted_b], axis=1).astype(jnp.bfloat16)


def dirichlet(fractions):
    bin_shift = jnp.arange(W, dtype=jnp.float32)
    distance = fractions[:, None] + (W // 2 - 1) - bin_shift[None, :]
    parity = (jnp.arange(W, dtype=jnp.int32) % 2).astype(jnp.float32)
    alternate = 1.0 - 2.0 * parity
    return (alternate[None, :] * jnp.sin(jnp.pi * fractions)[:, None] / (jnp.pi * distance)).astype(
        jnp.bfloat16
    )


def antenna_prefix(antenna):
    along_a = antenna[:, 0] * antenna[:, 0] + antenna[:, 1] * antenna[:, 1]
    along_b = antenna[:, 2] * antenna[:, 2] + antenna[:, 3] * antenna[:, 3]
    across = antenna[:, 0] * antenna[:, 2] + antenna[:, 1] * antenna[:, 3]
    stacked = jnp.stack([along_a, along_b, across], axis=1)
    return jnp.concatenate([jnp.zeros((1, 3), jnp.float32), jnp.cumsum(stacked, axis=0)], axis=0)


def statistic(interval, weights):
    real_a = interval[..., 0, :]
    imag_a = interval[..., 1, :]
    real_b = interval[..., 2, :]
    imag_b = interval[..., 3, :]
    weight_a = weights[..., 0:1]
    weight_b = weights[..., 1:2]
    weight_c = weights[..., 2:3]
    numerator = (
        weight_b * (real_a * real_a + imag_a * imag_a)
        + weight_a * (real_b * real_b + imag_b * imag_b)
        - 2.0 * weight_c * (real_a * real_b + imag_a * imag_b)
    )
    return numerator / (weight_a * weight_b - weight_c * weight_c)


def selector(places, band_width):
    bin_ids = jnp.arange(band_width, dtype=jnp.int32)
    return (places[..., None] == bin_ids).astype(jnp.bfloat16)


def body(spectra, offsets, fractions, antenna, starts, durations):
    block_count = offsets.shape[1]
    template_count = fractions.shape[0]
    block_width = template_count // block_count
    window_shift = jnp.arange(W, dtype=jnp.int32)
    band_count = lax.axis_size("tmpl")
    band_width = spectra.shape[2] // band_count
    owned_offsets = lax.all_to_all(offsets, "tmpl", split_axis=0, concat_axis=1, tiled=True)
    owned_rows = owned_offsets.shape[0]
    all_blocks = owned_offsets.shape[1]
    places = (owned_offsets[:, :, None] + window_shift[None, None, :]).reshape(
        owned_rows, band_count, block_count * W
    )
    picker = selector(places, band_width)
    split_bands = spectra.reshape(owned_rows, 4, band_count, band_width)
    chosen = jnp.einsum("sctn,stkn->stck", split_bands, picker, preferred_element_type=jnp.float32)
    chosen = chosen.astype(jnp.bfloat16).reshape(owned_rows, band_count, 4, block_count, W)
    flat_windows = jnp.transpose(chosen, (0, 2, 1, 3, 4)).reshape(owned_rows, 4, all_blocks * W)
    arrived = lax.all_to_all(flat_windows, "tmpl", split_axis=2, concat_axis=0, tiled=True)
    windows = arrived.reshape(arrived.shape[0], 4, block_count, W)
    sft_rows = windows.shape[0]
    time_block = lax.axis_index("tm")
    first_sft = time_block * sft_rows
    local_antenna = lax.dynamic_slice_in_dim(antenna, first_sft, sft_rows, 0)
    weighted = weigh(windows, local_antenna)
    kernel = dirichlet(fractions).reshape(block_count, block_width, W)
    atom_rows = jnp.einsum("scbm,bqm->sbcq", weighted, kernel, preferred_element_type=jnp.float32)
    feature_count = block_count * 4 * block_width
    atom_rows = atom_rows.reshape(sft_rows, feature_count)
    grid_size = starts.shape[0]
    my_rows = grid_size // lax.axis_size("tm")
    my_durations = lax.dynamic_slice_in_dim(durations, time_block * my_rows, my_rows, 0)
    end_points = starts[None, :] + my_durations[:, None]
    sft_global = first_sft + jnp.arange(sft_rows, dtype=jnp.int32)
    before_mask = (sft_global[None, :] < starts[:, None]).astype(jnp.float32)
    before = jnp.dot(before_mask, atom_rows, precision=lax.Precision.HIGHEST)
    chosen_ends = starts[None, :] + durations[:, None]
    through_mask = (sft_global[None, None, :] < chosen_ends[:, :, None]).astype(jnp.float32)
    through_mask = through_mask.reshape(my_rows * lax.axis_size("tm") * grid_size, sft_rows)
    through_end = jnp.dot(through_mask, atom_rows, precision=lax.Precision.HIGHEST)
    interval = lax.psum_scatter(
        through_end.reshape(my_rows * lax.axis_size("tm"), grid_size, feature_count) - before[None],
        "tm",
        scatter_dimension=0,
        tiled=True,
    )
    cum_weights = antenna_prefix(antenna)
    weights = cum_weights[end_points] - cum_weights[starts][None]
    split_interval = interval.reshape(my_rows, grid_size, block_count, 4, block_width)
    fstat_blocks = statistic(split_interval, weights[:, :, None, :])
    fstat_map = fstat_blocks.reshape(my_rows, grid_size, template_count)
    loudest = lax.pmax(jnp.max(fstat_map, axis=2), "tmpl")
    return (fstat_map, loudest)


def solution(mesh):
    in_specs = (
        P(("grp", "tm", "tmpl"), None, None),
        P(("grp", "tm"), "tmpl"),
        P(("grp", "tmpl")),
        P("grp", None),
        P("grp"),
        P("grp"),
    )
    out_specs = (P("tm", None, ("grp", "tmpl")), P(("grp", "tm"), None))
    return jax.shard_map(body, mesh=mesh, in_specs=in_specs, out_specs=out_specs, check_vma=False)
```

profile of v0, /device:TPU:0, one launch (start us, length us, event | category | flops | bytes accessed | tf_op | source)
XLA Modules:
  0.0 116.5 jit_solution(2259706734415102542)
XLA Ops:
  7.2 0.9 all_to_all.9
  8.1 0.6 copy.26
  8.7 7.3 %all-to-all-start = ((s32[8,32,2]{1,2,0:T(2,128)}), s32[8,32,2]{1,2,0:T(2,128)S(1)}, u32[]{:S(2)}, u32[]{:S(2)}) async-start(s32[8,32,2]{1,2,0:T(2,128)} %copy.26), calls=%async_computation | async-start | bytes 16384 | tf_op jit(solution)/shard_map/all_to_all | solution.py:70
  16.0 0.7 sine_bitcast_fusion
  16.7 0.7 broadcast_add_fusion
  17.5 5.0 %all-to-all-done = s32[8,32,2]{1,2,0:T(2,128)S(1)} async-done(((s32[8,32,2]{1,2,0:T(2,128)}), s32[8,32,2]{1,2,0:T(2,128)S(1)}, u32[]{:S(2)}, u32[]{:S(2)}) %all-to-all-start) | async-done | bytes 2080 | tf_op jit(solution)/shard_map/all_to_all | solution.py:70
  22.7 7.1 %fusion.3 = bf16[32,8,4,32]{3,2,1,0:T(4,128)(2,1)S(1)} fusion(bf16[32,4,8,1024]{3,1,2,0:T(4,128)(2,1)S(1)} %bitcast.67, s32[32,8,32]{2,1,0:T(8,128)S(1)} %copy.27), kind=kOutput, calls=%fused_computation.7 | convolution fusion | flops 75530240 | bytes 2195456 | tf_op jit(solution)/shard_map/sctn,stkn->stck/dot_general | solution.py:78
  30.3 0.9 reshape.267
  31.2 3.4 %all-to-all-start.1 = ((bf16[8,2,2048]{2,1,0:T(2,128)(2,1)}), bf16[8,2,2048]{2,1,0:T(2,128)(2,1)S(1)}, u32[]{:S(2)}, u32[]{:S(2)}) async-start(bf16[8,2,2048]{2,1,0:T(2,128)(2,1)} %reshape.267), calls=%async_computation.1 | async-start | bytes 131072 | tf_op jit(solution)/shard_map/all_to_all | solution.py:81
  34.8 6.7 %all-to-all-done.1 = bf16[8,2,2048]{2,1,0:T(2,128)(2,1)S(1)} async-done(((bf16[8,2,2048]{2,1,0:T(2,128)(2,1)}), bf16[8,2,2048]{2,1,0:T(2,128)(2,1)S(1)}, u32[]{:S(2)}, u32[]{:S(2)}) %all-to-all-start.1) | async-done | bytes 65568 | tf_op jit(solution)/shard_map/all_to_all | solution.py:81
  42.5 0.6 fusion.12
  43.1 3.8 %convolution_subtract_fusion = f32[32,32,1024]{2,1,0:T(8,128)} fusion(f32[256,1024,1]{0,1,2:T(8,128)S(1)} %bitcast.69, f32[32,1024]{1,0:T(8,128)S(1)} %fusion.12, s32[32,32]{1,0:T(8,128)S(1)} %broadcast_add_fusion, s32[256]{0:T(256)S(1)} %iota_add_fusion), kind=kOutput, calls=%fused_computation.5 | convolution fusion | flops 3222536192 | bytes 5379072 | tf_op jit(solution)/shard_map/dot_general | solution.py:102
  47.0 0.9 reduce-window.6
  48.8 1.0 gather_fusion
  50.1 0.6 gather_fusion.1
  50.7 5.9 %reduce-scatter.2.cloned.1.call-done = f32[16,32,1024]{2,1,0:T(8,128)} async-done(((f32[32,32,1024]{2,1,0:T(8,128)}), f32[16,32,1024]{2,1,0:T(8,128)}) %reduce-scatter.2.cloned.1.call-update) | async-done | bytes 2097168 | tf_op jit(solution)/shard_map/reduce_scatter | solution.py:103
  56.7 3.2 %reshape.219 = f32[16,32,2,4,128]{4,3,2,1,0:T(4,128)} reshape(f32[16,32,1024]{2,1,0:T(8,128)} %reduce-scatter.2.cloned.1.call-done) | data formatting | bytes 4194304 | tf_op jit(solution)/shard_map/reshape | solution.py:111
  59.9 6.7 %multiply_add_fusion.2 = (f32[16,32,2,1,128]{4,3,2,1,0:T(1,128)S(1)}, f32[16,32,2,1,128]{4,3,2,1,0:T(1,128)S(1)}, f32[16,32,2,1,128]{4,3,2,1,0:T(1,128)}) fusion(f32[16,32,2,4,128]{4,3,2,1,0:T(4,128)} %reshape.219), kind=kLoop, calls=%fused_computation.14 | loop fusion | flops 1179648 | bytes 3670016 | tf_op jit(solution)/shard_map/add | solution.py:51
  67.1 12.7 %fusion.7 = (f32[16,32]{1,0:T(8,128)S(1)}, f32[16,32,2,128]{3,2,1,0:T(2,128)}, f32[16,32,2,128]{3,2,1,0:T(2,128)}, f32[16,32,2,128]{3,2,1,0:T(2,128)}) fusion(f32[16,32,2,1,128]{4,3,2,1,0:T(1,128)S(1)} %get-tuple-element.7, f32[16,32,2,1,128]{4,3,2,1,0:T(1,128)} %get-tuple-element.8, f32[16,32,2,1,128]{4,3,2,1,0:T(1,128)S(1)} %get-tuple-element.6, ...), kind=kLoop, calls=%fused_computation.17 | loop fusion | flops 916992 | bytes 3155972 | tf_op jit(solution)/shard_map/reduce_max | solution.py:114
  79.8 1.5 %add.201 = f32[16,32,256]{2,1,0:T(8,128)S(1)} reshape(f32[16,32,2,128]{3,2,1,0:T(2,128)} %get-tuple-element.3) | data formatting | bytes 1048576 | tf_op jit(solution)/shard_map/add | solution.py:51
  81.3 1.5 %add.203 = f32[16,32,256]{2,1,0:T(8,128)S(1)} reshape(f32[16,32,2,128]{3,2,1,0:T(2,128)} %get-tuple-element.4) | data formatting | bytes 1048576 | tf_op jit(solution)/shard_map/add | solution.py:52
  82.7 2.3 %add.206 = f32[16,32,256]{2,1,0:T(8,128)} reshape(f32[16,32,2,128]{3,2,1,0:T(2,128)} %get-tuple-element.5) | data formatting | bytes 1048576 | tf_op jit(solution)/shard_map/add | solution.py:53
  85.0 22.5 %pmax.7 = f32[16,32]{1,0:T(8,128)} all-reduce(f32[16,32]{1,0:T(8,128)S(1)} %get-tuple-element.2), channel_id=1, replica_groups=mesh['grp'=2,'tmpl'=8,'tm'=2] {'tmpl'}, use_global_device_ids=true, to_apply=%region_4.5 | all-reduce | flops 512 | bytes 4096 | tf_op jit(solution)/shard_map/pmax | solution.py:114
  107.5 2.2 %subtract_divide_fusion.1 = f32[16,32,256]{2,1,0:T(8,128)} fusion(f32[16,32,256]{2,1,0:T(8,128)} %add.206, f32[16,32,256]{2,1,0:T(8,128)S(1)} %add.203, f32[16,32,256]{2,1,0:T(8,128)S(1)} %add.201, f32[16,32]{1,0:T(8,128)S(1)} %get-tuple-element.14, f32[16,32]{1,0:T(8,128)S(1)} %get-tuple-element.15, f32[16,32]{1,0:T(8,128)S(1)} %get-tuple-element.16, ...), kind=kLoop, calls=%fused_computation.11 | loop fusion | flops 786432 | bytes 2105344 | tf_op jit(solution)/shard_map/div | solution.py:55
  (45 shorter events, 3.6 us)
Async XLA Ops:
  7.2 15.5 %copy-start = (bf16[32,4,8192]{2,1,0:T(4,128)(2,1)S(1)}, bf16[32,4,8192]{2,1,0:T(4,128)(2,1)}, u32[]{:S(2)}) copy-start(bf16[32,4,8192]{2,1,0:T(4,128)(2,1)} %param.6) | copy-start | bytes 6291460
  8.7 13.8 %all-to-all-start = ((s32[8,32,2]{1,2,0:T(2,128)}), s32[8,32,2]{1,2,0:T(2,128)S(1)}, u32[]{:S(2)}, u32[]{:S(2)}) async-start(s32[8,32,2]{1,2,0:T(2,128)} %copy.26), calls=%async_computation | async-start | bytes 16384 | tf_op jit(solution)/shard_map/all_to_all | solution.py:70
  22.7 12.0 %copy-start.1 = (f32[512,4]{0,1:T(4,128)S(1)}, f32[512,4]{0,1:T(4,128)}, u32[]{:S(2)}) copy-start(f32[512,4]{0,1:T(4,128)} %param.9) | copy-start | bytes 24580
  29.8 12.7 %copy-start.2 = (s32[32]{0:T(128)S(1)}, s32[32]{0:T(128)}, u32[]{:S(2)}) copy-start(s32[32]{0:T(128)} %param.10) | copy-start | bytes 388
  31.2 10.2 %all-to-all-start.1 = ((bf16[8,2,2048]{2,1,0:T(2,128)(2,1)}), bf16[8,2,2048]{2,1,0:T(2,128)(2,1)S(1)}, u32[]{:S(2)}, u32[]{:S(2)}) async-start(bf16[8,2,2048]{2,1,0:T(2,128)(2,1)} %reshape.267), calls=%async_computation.1 | async-start | bytes 131072 | tf_op jit(solution)/shard_map/all_to_all | solution.py:81
  34.6 22.1 %reduce-scatter.2.cloned.1.call-start = ((), (), s32[]{:S(2)}) async-start(), calls=%async_computation.3 | async-start | bytes 6291456 | tf_op jit(solution)/shard_map/reduce_scatter | solution.py:103
  43.1 5.5 %copy-start.3 = (s32[32]{0:T(128)S(1)}, s32[32]{0:T(128)}, u32[]{:S(2)}) copy-start(s32[32]{0:T(128)} %param.11) | copy-start | bytes 388
Sparse Core Ops, SparseCore 0:
  47.1 9.5 reduce-scatter.1
where the time goes:
time: 117 us
  other arithmetic  24.5 us (21%)
  blocking collectives  22.5 us (19%)
  waiting for transfers between devices  17.6 us (15%)
  local copies, waits for them, and re-layouts  15.1 us (13%)
  between operations  14.2 us (12%)
  matrix products  11.9 us (10%)
  starting transfers between devices  10.7 us (9%)
    pmax x1, blocking collectives, body(): loudest = lax.pmax(jnp.max(fstat_map, axis=2), 'tmpl')  22.5 us
    reduce_max x1, other arithmetic, body(): loudest = lax.pmax(jnp.max(fstat_map, axis=2), 'tmpl')  12.7 us
    all_to_all x1, starting transfers between devices, body(): lax.all_to_all(offsets, 'tmpl', split_axis=0, concat_axis=1, tiled=True)  7.28 us
    dot_general x1, matrix products, body(): jnp.einsum('sctn,stkn->stck', split_bands, picker, preferred_element_type...  7.05 us
    all_to_all x1, waiting for transfers between devices, body(): lax.all_to_all(flat_windows, 'tmpl', split_axis=2, concat_axis=0, tiled=T...  6.68 us
    add x1, other arithmetic, statistic(): real_a * real_a + imag_a * imag_a  6.67 us
    reduce_scatter x1, waiting for transfers between devices, body(): lax.psum_scatter(through_end.reshape(my_rows * lax.axis_size('tm'), grid_...  5.92 us
    all_to_all x1, waiting for transfers between devices, body(): lax.all_to_all(offsets, 'tmpl', split_axis=0, concat_axis=1, tiled=True)  4.96 us
  transfers between devices with their start and end apart: 3, of which 3 were waited for; matrix products, arithmetic and copies ran while one was open for 5% of the time, Pallas kernels for 0%

commit v1 on v0

v1 whole, which is shorter than its diff:
```python
import functools

import jax
import jax.numpy as jnp
from jax import lax
from jax.experimental import pallas as pl
from jax.experimental.pallas import tpu as pltpu
from jax.sharding import PartitionSpec as P

W = 16
LANES = 128
F32 = jnp.float32
BF16 = jnp.bfloat16
MESH = pl.DeviceIdType.MESH


def split3(x):
    hi = x.astype(BF16)
    rest = x - hi.astype(F32)
    mid = rest.astype(BF16)
    return hi, mid, (rest - mid.astype(F32)).astype(BF16)


def fused(
    cfg,
    off_ref, spec_ref, frac_ref, ant_ref, starts_ref, dur_ref,
    fstat_ref, loud_ref,
    xbuf, xf, off_send, off_recv, wsend, wall, mask, lsend, lrecv,
    spec_sem, osend_sem, orecv_sem, wsend_sem, wrecv_sem, lsend_sem, lrecv_sem,
):
    bands, times, rows, nb, chunks, nsft, grid, my_rows = cfg
    t_me = lax.axis_index("tmpl")
    m_me = lax.axis_index("tm")
    group = bands * times
    me = m_me * bands + t_me

    spec_copy = pltpu.make_async_copy(spec_ref, xbuf, spec_sem)
    spec_copy.start()

    barrier = pltpu.get_barrier_semaphore()

    def greet(k, carry):
        peer = lax.rem(me + k, group)
        pl.semaphore_signal(
            barrier, inc=1,
            device_id={"tmpl": lax.rem(peer, bands), "tm": lax.div(peer, bands)},
            device_id_type=MESH,
        )
        return carry

    lax.fori_loop(1, group, greet, 0)

    off_send[...] = jnp.zeros_like(off_send)
    for t in range(bands):
        off_send[t, 0:nb, 0:rows] = off_ref[:, t * rows:(t + 1) * rows]
    off_recv[t_me] = off_send[t_me]
    pl.semaphore_wait(barrier, group - 1)

    def off_copy(k):
        peer = lax.rem(t_me + k, bands)
        return pltpu.make_async_remote_copy(
            src_ref=off_send.at[peer], dst_ref=off_recv.at[t_me],
            send_sem=osend_sem.at[peer], recv_sem=orecv_sem.at[t_me],
            device_id={"tmpl": peer}, device_id_type=MESH,
        )

    def off_arrival(k):
        source = lax.rem(t_me + k, bands)
        return pltpu.make_async_remote_copy(
            src_ref=off_send.at[source], dst_ref=off_recv.at[source],
            send_sem=osend_sem.at[source], recv_sem=orecv_sem.at[source],
            device_id={"tmpl": source}, device_id_type=MESH,
        )

    def start_off(k, carry):
        off_copy(k).start()
        return carry

    lax.fori_loop(1, bands, start_off, 0)

    spec_copy.wait()

    def widen(i, carry):
        pair = jnp.concatenate(
            [xbuf[2 * i].astype(F32), xbuf[2 * i + 1].astype(F32)], axis=0
        )
        at = pl.ds(pl.multiple_of(i * 8, 8), 8)
        for ch in range(bands * chunks):
            xf[ch, at, :] = pair[:, ch * LANES:(ch + 1) * LANES]
        return carry

    lax.fori_loop(0, rows // 2, widen, 0)

    lane = lax.broadcasted_iota(jnp.int32, (rows, LANES), 1)
    lane_m = lane % W
    lane_b = (lane // W) % nb
    lane_c = lane // (W * nb)
    ant_t = jnp.transpose(
        jnp.concatenate([ant_ref[...], jnp.zeros((4, nsft), F32)], axis=0)
    )
    mine = jnp.zeros((rows, 8), F32)
    for slot in range(group):
        mine = jnp.where(slot == me, ant_t[slot * rows:(slot + 1) * rows, :], mine)
    upper = lane_c < 2
    coef_p = jnp.where(upper, mine[:, 0:1], mine[:, 2:3])
    coef_q = jnp.where(upper, mine[:, 1:2], mine[:, 3:4])
    even = (lane_c % 2) == 0

    def window_copy(t, m):
        return pltpu.make_async_remote_copy(
            src_ref=wsend.at[t], dst_ref=wall.at[me],
            send_sem=wsend_sem.at[m * bands + t], recv_sem=wrecv_sem.at[me],
            device_id={"tmpl": t, "tm": m}, device_id_type=MESH,
        )

    def pick(k, carry):
        t = lax.rem(t_me + k, bands)

        @pl.when(k < bands)
        def _():
            off_arrival(k).wait_recv()

        columns = jnp.transpose(off_recv[t])[0:rows, :]
        place = jnp.zeros((rows, LANES), jnp.int32)
        for b in range(nb):
            place = jnp.where(lane_b == b, columns[:, b:b + 1], place)
        place = place + lane_m
        chunk = place // LANES
        spot = place % LANES
        picked = [jnp.zeros((rows, LANES), F32) for _ in range(4)]
        for ch in range(chunks):
            here = chunk == ch
            for c in range(4):
                piece = xf[t * chunks + ch, pl.ds(c, rows, stride=4), :]
                got = jnp.take_along_axis(piece, spot, axis=1, mode="promise_in_bounds")
                picked[c] = jnp.where(here, got, picked[c])
        one = jnp.where(even, picked[0], picked[1])
        two = jnp.where(even, picked[2], picked[3])
        wsend[t] = (coef_p * one + coef_q * two).astype(BF16)
        for m in range(times):
            @pl.when(jnp.logical_or(t != t_me, m != m_me))
            def _():
                window_copy(t, m).start()
        return carry

    lax.fori_loop(1, bands + 1, pick, 0)
    wall[me] = wsend[t_me]

    row = lax.broadcasted_iota(jnp.int32, (grid, LANES), 0)
    begin = jnp.zeros((grid, LANES), jnp.int32)
    for i in range(grid):
        begin = jnp.where(row == i, starts_ref[i], begin)
    begin = jnp.concatenate([begin] * (nsft // LANES), axis=1)
    sft = lax.broadcasted_iota(jnp.int32, (grid, nsft), 1)
    since = sft - begin
    for j in range(my_rows):
        length = dur_ref[m_me * my_rows + j]
        inside = jnp.logical_and(since >= 0, since < length)
        mask[j * grid:(j + 1) * grid, :] = inside.astype(F32).astype(BF16)

    ant = ant_ref[...]
    a1, a2, b1, b2 = ant[0:1], ant[1:2], ant[2:3], ant[3:4]
    terms = jnp.concatenate(
        [a1 * a1 + a2 * a2, b1 * b1 + b2 * b2, a1 * b1 + a2 * b2, jnp.zeros((5, nsft), F32)],
        axis=0,
    )
    nt = (((1,), (1,)), ((), ()))
    sums = 0.0
    for piece in split3(terms):
        sums = sums + lax.dot_general(mask[...], piece, nt, preferred_element_type=F32)

    width = frac_ref.shape[1]
    fracs = frac_ref[...]
    shift = lax.broadcasted_iota(jnp.int32, (W, width), 0)
    alternate = (1 - 2 * (shift % 2)).astype(F32)
    distance = fracs + (W // 2 - 1) - shift.astype(F32)
    dirichlet = alternate * jnp.sin(jnp.pi * fracs) / (jnp.pi * distance)
    tiled = jnp.concatenate([dirichlet] * (4 * nb), axis=0)
    feature = lax.broadcasted_iota(jnp.int32, tiled.shape, 0)
    block = lax.broadcasted_iota(jnp.int32, tiled.shape, 1) // (width // nb)
    same = (feature // W) % nb == block
    bases = []
    for c in range(4):
        base = jnp.where(jnp.logical_and(same, feature // (W * nb) == c), tiled, 0.0)
        base = base.astype(BF16)
        bases.append(jnp.concatenate([base, base], axis=0))

    def window_arrival(k):
        source = lax.rem(me + k, group)
        return pltpu.make_async_remote_copy(
            src_ref=wsend.at[0], dst_ref=wall.at[source],
            send_sem=wsend_sem.at[source], recv_sem=wrecv_sem.at[source],
            device_id={"tmpl": lax.rem(source, bands), "tm": lax.div(source, bands)},
            device_id_type=MESH,
        )

    def arrive(k, carry):
        window_arrival(k).wait_recv()
        return carry

    lax.fori_loop(1, group, arrive, 0)
    everything = wall[...].reshape(nsft, LANES)

    step = 128
    for r in range(my_rows * grid // step):
        at = slice(r * step, (r + 1) * step)
        total = jnp.dot(mask[at, :], everything, preferred_element_type=F32)
        hi = total.astype(BF16)
        lo = (total - hi.astype(F32)).astype(BF16)
        both = jnp.concatenate([hi, lo], axis=1)
        ra, ia, rb, ib = [jnp.dot(both, base, preferred_element_type=F32) for base in bases]
        wa, wb, wc = sums[at, 0:1], sums[at, 1:2], sums[at, 2:3]
        inverse = 1.0 / (wa * wb - wc * wc)
        top = wb * (ra * ra + ia * ia) + wa * (rb * rb + ib * ib) - (2.0 * wc) * (ra * rb + ia * ib)
        stat = top * inverse
        fstat_ref[at, :] = stat
        best = stat[:, 0:LANES]
        for q in range(1, width // LANES):
            best = jnp.maximum(best, stat[:, q * LANES:(q + 1) * LANES])
        lsend[0:1, at] = jnp.max(jnp.transpose(best), axis=0, keepdims=True)

    def loud_copy(k):
        peer = lax.rem(t_me + k, bands)
        return pltpu.make_async_remote_copy(
            src_ref=lsend, dst_ref=lrecv.at[t_me],
            send_sem=lsend_sem.at[peer], recv_sem=lrecv_sem.at[t_me],
            device_id={"tmpl": peer}, device_id_type=MESH,
        )

    def loud_arrival(k):
        source = lax.rem(t_me + k, bands)
        return pltpu.make_async_remote_copy(
            src_ref=lsend, dst_ref=lrecv.at[source],
            send_sem=lsend_sem.at[source], recv_sem=lrecv_sem.at[source],
            device_id={"tmpl": source}, device_id_type=MESH,
        )

    def start_loud(k, carry):
        loud_copy(k).start()
        return carry

    lax.fori_loop(1, bands, start_loud, 0)

    def window_done(k, carry):
        peer = lax.rem(me + k, group)
        window_copy(lax.rem(peer, bands), lax.div(peer, bands)).wait_send()
        return carry

    lax.fori_loop(1, group, window_done, 0)

    def off_done(k, carry):
        off_copy(k).wait_send()
        return carry

    lax.fori_loop(1, bands, off_done, 0)
    lrecv[t_me] = lsend[...]

    def loud_arrive(k, carry):
        loud_arrival(k).wait_recv()
        return carry

    lax.fori_loop(1, bands, loud_arrive, 0)
    most = lrecv[0]
    for t in range(1, bands):
        most = jnp.maximum(most, lrecv[t])
    for j in range(my_rows):
        loud_ref[j:j + 1, :] = most[:, j * grid:(j + 1) * grid]

    def loud_done(k, carry):
        loud_copy(k).wait_send()
        return carry

    lax.fori_loop(1, bands, loud_done, 0)


def body(spectra, offsets, fractions, antenna, starts, durations):
    bands = lax.axis_size("tmpl")
    times = lax.axis_size("tm")
    rows, _, bins = spectra.shape
    nb = offsets.shape[1]
    width = fractions.shape[0]
    nsft = antenna.shape[0]
    grid = starts.shape[0]
    my_rows = grid // times
    chunks = bins // bands // LANES
    group = bands * times
    cells = my_rows * grid
    cfg = (bands, times, rows, nb, chunks, nsft, grid, my_rows)
    vmem = pl.BlockSpec(memory_space=pltpu.VMEM)
    smem = pl.BlockSpec(memory_space=pltpu.SMEM)
    fstat, loudest = pl.pallas_call(
        functools.partial(fused, cfg),
        out_shape=(
            jax.ShapeDtypeStruct((cells, width), F32),
            jax.ShapeDtypeStruct((my_rows, grid), F32),
        ),
        in_specs=[vmem, pl.BlockSpec(memory_space=pl.ANY), vmem, vmem, smem, smem],
        out_specs=(vmem, vmem),
        scratch_shapes=[
            pltpu.VMEM((rows, 4, bins), BF16),
            pltpu.VMEM((bins // LANES, rows * 4, LANES), F32),
            pltpu.VMEM((bands, 8, LANES), jnp.int32),
            pltpu.VMEM((bands, 8, LANES), jnp.int32),
            pltpu.VMEM((bands, rows, LANES), BF16),
            pltpu.VMEM((group, rows, LANES), BF16),
            pltpu.VMEM((cells, nsft), BF16),
            pltpu.VMEM((1, cells), F32),
            pltpu.VMEM((bands, 1, cells), F32),
            pltpu.SemaphoreType.DMA,
            pltpu.SemaphoreType.DMA((bands,)),
            pltpu.SemaphoreType.DMA((bands,)),
            pltpu.SemaphoreType.DMA((group,)),
            pltpu.SemaphoreType.DMA((group,)),
            pltpu.SemaphoreType.DMA((bands,)),
            pltpu.SemaphoreType.DMA((bands,)),
        ],
        compiler_params=pltpu.CompilerParams(
            collective_id=0, has_side_effects=True, vmem_limit_bytes=40 * 1024 * 1024
        ),
        name="transient_fstat",
    )(offsets.T, spectra, fractions.reshape(1, width), antenna.T, starts, durations)
    return fstat.reshape(my_rows, grid, width), loudest


def solution(mesh):
    in_specs = (
        P(("grp", "tm", "tmpl"), None, None),
        P(("grp", "tm"), "tmpl"),
        P(("grp", "tmpl")),
        P("grp", None),
        P("grp"),
        P("grp"),
    )
    out_specs = (P("tm", None, ("grp", "tmpl")), P(("grp", "tm"), None))
    return jax.shard_map(body, mesh=mesh, in_specs=in_specs, out_specs=out_specs, check_vma=False)
```

time: 117 us -> 30 us (0.26)
  other arithmetic: 24.5 us -> 0 us
  Pallas kernels: 0 us -> 22.7 us
  blocking collectives: 22.5 us -> 0 us
  waiting for transfers between devices: 17.6 us -> 0 us
  between operations: 14.2 us -> 0.65 us
  matrix products: 11.9 us -> 0 us
  starting transfers between devices: 10.7 us -> 0 us
  local copies, waits for them, and re-layouts: 15.1 us -> 6.34 us
    pallas_call x0 -> x1, Pallas kernels: none -> 22.7 us  [body(): pl.pallas_call(functools.partial(fused, cfg), out_shape=(jax.ShapeDtypeSt...]
    pmax x1 -> x0, blocking collectives: 22.5 us -> none  [body(): loudest = lax.pmax(jnp.max(fstat_map, axis=2), 'tmpl')]
    reduce_max x1 -> x0, other arithmetic: 12.7 us -> none  [body(): loudest = lax.pmax(jnp.max(fstat_map, axis=2), 'tmpl')]
    dot_general x4 -> x0, matrix products: 11.9 us -> none  [the longest x1 7.05 us: body(): jnp.einsum('sctn,stkn->stck', split_bands, picker, preferred_element_type...]
    all_to_all x2 -> x0, waiting for transfers between devices: 11.6 us -> none  [the longest x1 6.68 us: body(): lax.all_to_all(flat_windows, 'tmpl', split_axis=2, concat_axis=0, tiled=T...]
    all_to_all x2 -> x0, starting transfers between devices: 10.6 us -> none  [the longest x1 7.28 us: body(): lax.all_to_all(offsets, 'tmpl', split_axis=0, concat_axis=1, tiled=True)]
    add x5 -> x0, other arithmetic: 7.51 us -> none  [the longest x1 6.67 us: statistic(): real_a * real_a + imag_a * imag_a]
    reduce_scatter x1 -> x0, waiting for transfers between devices: 5.92 us -> none  [body(): lax.psum_scatter(through_end.reshape(my_rows * lax.axis_size('tm'), grid_...]
  transfers between devices with their start and end apart: 3 -> 0, of which waited for: 3 -> 0; matrix products, arithmetic and copies ran while one was open for 5% -> 0% of each run, Pallas kernels for 0% -> 0%
where the time goes in v1:
time: 30 us; the launch traced here: 29.7 us
  Pallas kernels  22.7 us (76%)
  local copies, waits for them, and re-layouts  6.34 us (21%)
  between operations  0.65 us (2%)
    pallas_call x1, Pallas kernels, body(): pl.pallas_call(functools.partial(fused, cfg), out_shape=(jax.ShapeDtypeSt...  22.7 us
    unnamed x14, local copies, waits for them, and re-layouts  6.34 us

profile of v1, /device:TPU:0, one launch (start us, length us, event | category | flops | bytes accessed | tf_op | source)
XLA Modules:
  0.0 29.7 jit_solution(9084325563967046176)
XLA Ops:
  0.6 0.0 copy-start
  0.6 1.6 %copy-done = bf16[32,4,8192]{2,1,0:T(4,128)(2,1)S(1)} copy-done((bf16[32,4,8192]{2,1,0:T(4,128)(2,1)S(1)}, bf16[32,4,8192]{2,1,0:T(4,128)(2,1)}, u32[]{:S(2)}) %copy-start) | copy-done | bytes 2097176
  2.2 0.0 copy-start.1
  2.2 0.7 %copy-done.1 = f32[512,4]{0,1:T(4,128)S(1)} copy-done((f32[512,4]{0,1:T(4,128)S(1)}, f32[512,4]{0,1:T(4,128)}, u32[]{:S(2)}) %copy-start.1) | copy-done | bytes 8216
  2.9 0.0 copy-start.2
  2.9 0.7 %copy-done.2 = s32[256,2]{0,1:T(2,128)S(1)} copy-done((s32[256,2]{0,1:T(2,128)S(1)}, s32[256,2]{0,1:T(2,128)}, u32[]{:S(2)}) %copy-start.2) | copy-done | bytes 2072
  3.6 0.0 copy-start.3
  3.6 0.7 %copy-done.3 = f32[256]{0:T(256)S(1)} copy-done((f32[256]{0:T(256)S(1)}, f32[256]{0:T(256)}, u32[]{:S(2)}) %copy-start.3) | copy-done | bytes 1048
  4.3 0.0 copy-start.4
  4.3 0.7 %copy-done.4 = s32[32]{0:T(128)S(1)} copy-done((s32[32]{0:T(128)S(1)}, s32[32]{0:T(128)}, u32[]{:S(2)}) %copy-start.4) | copy-done | bytes 152
  4.9 0.0 copy-start.5
  4.9 0.7 %copy-done.5 = s32[32]{0:T(128)S(1)} copy-done((s32[32]{0:T(128)S(1)}, s32[32]{0:T(128)}, u32[]{:S(2)}) %copy-start.5) | copy-done | bytes 152
  5.6 22.7 %transient_fstat.1 = (f32[512,256]{1,0:T(8,128)S(1)}, f32[16,32]{1,0:T(8,128)S(1)}) custom-call(s32[2,256]{1,0:T(2,128)S(1)} %bitcast.6, bf16[32,4,8192]{2,1,0:T(4,128)(2,1)S(1)} %copy-done, f32[1,256]{1,0:T(1,128)S(1)} %bitcast.7, f32[4,512]{1,0:T(4,128)S(1)} %bitcast.5, s32[32]{0:T(128)S(1)} %copy-done.4, s32[32]{0:T(128)S(1)} %copy-done.5), custom_call_target="tpu_custom_call" | custom-call | tf_op jit(solution)/shard_map/transient_fstat/pallas_call | solution.py:291
  28.3 0.8 %copy.10 = f32[16,32,256]{2,1,0:T(8,128)} copy(f32[16,32,256]{2,1,0:T(8,128)S(1)} %bitcast.4) | data formatting | bytes 1048576
  29.1 0.6 %copy.11 = f32[16,32]{1,0:T(8,128)} copy(f32[16,32]{1,0:T(8,128)S(1)} %get-tuple-element.9) | data formatting | bytes 4096
Async XLA Ops:
  0.6 1.6 %copy-start = (bf16[32,4,8192]{2,1,0:T(4,128)(2,1)S(1)}, bf16[32,4,8192]{2,1,0:T(4,128)(2,1)}, u32[]{:S(2)}) copy-start(bf16[32,4,8192]{2,1,0:T(4,128)(2,1)} %spec_ref.1) | copy-start | bytes 6291460
  2.2 0.7 %copy-start.1 = (f32[512,4]{0,1:T(4,128)S(1)}, f32[512,4]{0,1:T(4,128)}, u32[]{:S(2)}) copy-start(f32[512,4]{0,1:T(4,128)} %param.9) | copy-start | bytes 24580
  2.9 0.7 %copy-start.2 = (s32[256,2]{0,1:T(2,128)S(1)}, s32[256,2]{0,1:T(2,128)}, u32[]{:S(2)}) copy-start(s32[256,2]{0,1:T(2,128)} %param.7) | copy-start | bytes 6148
  3.6 0.7 %copy-start.3 = (f32[256]{0:T(256)S(1)}, f32[256]{0:T(256)}, u32[]{:S(2)}) copy-start(f32[256]{0:T(256)} %param.8) | copy-start | bytes 3076
  4.3 0.7 %copy-start.4 = (s32[32]{0:T(128)S(1)}, s32[32]{0:T(128)}, u32[]{:S(2)}) copy-start(s32[32]{0:T(128)} %starts_ref.1) | copy-start | bytes 388
  4.9 0.7 %copy-start.5 = (s32[32]{0:T(128)S(1)}, s32[32]{0:T(128)}, u32[]{:S(2)}) copy-start(s32[32]{0:T(128)} %dur_ref.1) | copy-start | bytes 388

commit v2 on v1

--- a/solution.py
+++ b/solution.py
@@ -23,8 +23,9 @@
 
 def fused(
     cfg,
-    off_ref, spec_ref, frac_ref, ant_ref, starts_ref, dur_ref,
-    fstat_ref, loud_ref,
+    off_in, spec_ref, frac_in, ant_in, starts_in, dur_in,
+    fstat_out, loud_ref,
+    off_ref, frac_ref, ant_ref, starts_ref, dur_ref, fstat_ref, small_sem, fstat_sem,
     xbuf, xf, off_send, off_recv, wsend, wall, mask, lsend, lrecv,
     spec_sem, osend_sem, orecv_sem, wsend_sem, wrecv_sem, lsend_sem, lrecv_sem,
 ):
@@ -35,6 +36,14 @@
     me = m_me * bands + t_me
 
     spec_copy = pltpu.make_async_copy(spec_ref, xbuf, spec_sem)
+    small = [
+        pltpu.make_async_copy(source, target, small_sem.at[n])
+        for n, (source, target) in enumerate(
+            [(off_in, off_ref), (starts_in, starts_ref), (dur_in, dur_ref), (ant_in, ant_ref), (frac_in, frac_ref)]
+        )
+    ]
+    for copy in small:
+        copy.start()
     spec_copy.start()
 
     barrier = pltpu.get_barrier_semaphore()
@@ -50,10 +59,26 @@
 
     lax.fori_loop(1, group, greet, 0)
 
+    small[0].wait()
     off_send[...] = jnp.zeros_like(off_send)
     for t in range(bands):
         off_send[t, 0:nb, 0:rows] = off_ref[:, t * rows:(t + 1) * rows]
     off_recv[t_me] = off_send[t_me]
+    small[1].wait()
+    small[2].wait()
+    row = lax.broadcasted_iota(jnp.int32, (grid, LANES), 0)
+    begin = jnp.zeros((grid, LANES), jnp.int32)
+    for i in range(grid):
+        begin = jnp.where(row == i, starts_ref[i], begin)
+    begin = jnp.concatenate([begin] * (nsft // LANES), axis=1)
+    sft = lax.broadcasted_iota(jnp.int32, (grid, nsft), 1)
+    since = sft - begin
+    for j in range(my_rows):
+        length = dur_ref[m_me * my_rows + j]
+        inside = jnp.logical_and(since >= 0, since < length)
+        mask[j * grid:(j + 1) * grid, :] = inside.astype(F32).astype(BF16)
+    small[3].wait()
+    small[4].wait()
     pl.semaphore_wait(barrier, group - 1)
 
     def off_copy(k):
@@ -146,18 +171,6 @@
     lax.fori_loop(1, bands + 1, pick, 0)
     wall[me] = wsend[t_me]
 
-    row = lax.broadcasted_iota(jnp.int32, (grid, LANES), 0)
-    begin = jnp.zeros((grid, LANES), jnp.int32)
-    for i in range(grid):
-        begin = jnp.where(row == i, starts_ref[i], begin)
-    begin = jnp.concatenate([begin] * (nsft // LANES), axis=1)
-    sft = lax.broadcasted_iota(jnp.int32, (grid, nsft), 1)
-    since = sft - begin
-    for j in range(my_rows):
-        length = dur_ref[m_me * my_rows + j]
-        inside = jnp.logical_and(since >= 0, since < length)
-        mask[j * grid:(j + 1) * grid, :] = inside.astype(F32).astype(BF16)
-
     ant = ant_ref[...]
     a1, a2, b1, b2 = ant[0:1], ant[1:2], ant[2:3], ant[3:4]
     terms = jnp.concatenate(
@@ -202,6 +215,11 @@
     everything = wall[...].reshape(nsft, LANES)
 
     step = 128
+
+    def fstat_copy(r):
+        part = pl.ds(r * step, step)
+        return pltpu.make_async_copy(fstat_ref.at[part], fstat_out.at[part], fstat_sem.at[r])
+
     for r in range(my_rows * grid // step):
         at = slice(r * step, (r + 1) * step)
         total = jnp.dot(mask[at, :], everything, preferred_element_type=F32)
@@ -214,6 +232,7 @@
         top = wb * (ra * ra + ia * ia) + wa * (rb * rb + ib * ib) - (2.0 * wc) * (ra * rb + ia * ib)
         stat = top * inverse
         fstat_ref[at, :] = stat
+        fstat_copy(r).start()
         best = stat[:, 0:LANES]
         for q in range(1, width // LANES):
             best = jnp.maximum(best, stat[:, q * LANES:(q + 1) * LANES])
@@ -271,6 +290,8 @@
         return carry
 
     lax.fori_loop(1, bands, loud_done, 0)
+    for r in range(my_rows * grid // step):
+        fstat_copy(r).wait()
 
 
 def body(spectra, offsets, fractions, antenna, starts, durations):
@@ -287,16 +308,24 @@
     cells = my_rows * grid
     cfg = (bands, times, rows, nb, chunks, nsft, grid, my_rows)
     vmem = pl.BlockSpec(memory_space=pltpu.VMEM)
-    smem = pl.BlockSpec(memory_space=pltpu.SMEM)
+    anywhere = pl.BlockSpec(memory_space=pl.ANY)
     fstat, loudest = pl.pallas_call(
         functools.partial(fused, cfg),
         out_shape=(
             jax.ShapeDtypeStruct((cells, width), F32),
             jax.ShapeDtypeStruct((my_rows, grid), F32),
         ),
-        in_specs=[vmem, pl.BlockSpec(memory_space=pl.ANY), vmem, vmem, smem, smem],
-        out_specs=(vmem, vmem),
+        in_specs=[anywhere] * 6,
+        out_specs=(anywhere, vmem),
         scratch_shapes=[
+            pltpu.VMEM((nb, offsets.shape[0]), jnp.int32),
+            pltpu.VMEM((1, width), F32),
+            pltpu.VMEM((4, nsft), F32),
+            pltpu.SMEM((grid,), jnp.int32),
+            pltpu.SMEM((grid,), jnp.int32),
+            pltpu.VMEM((cells, width), F32),
+            pltpu.SemaphoreType.DMA((5,)),
+            pltpu.SemaphoreType.DMA((cells // 128,)),
             pltpu.VMEM((rows, 4, bins), BF16),
             pltpu.VMEM((bins // LANES, rows * 4, LANES), F32),
             pltpu.VMEM((bands, 8, LANES), jnp.int32),
@@ -315,7 +344,7 @@
             pltpu.SemaphoreType.DMA((bands,)),
         ],
         compiler_params=pltpu.CompilerParams(
-            collective_id=0, has_side_effects=True, vmem_limit_bytes=40 * 1024 * 1024
+            collective_id=0, has_side_effects=True, vmem_limit_bytes=60 * 1024 * 1024
         ),
         name="transient_fstat",
     )(offsets.T, spectra, fractions.reshape(1, width), antenna.T, starts, durations)

time: 30 us -> 26.8 us (0.89)
  local copies, waits for them, and re-layouts: 6.34 us -> 3.18 us
    unnamed x14 -> x2, local copies, waits for them, and re-layouts: 6.34 us -> 3.18 us
where the time goes in v2:
time: 26.8 us; the launch traced here: 26.5 us
  Pallas kernels  22.7 us (85%)
  local copies, waits for them, and re-layouts  3.18 us (12%)
  between operations  0.64 us (2%)
    pallas_call x1, Pallas kernels, body(): pl.pallas_call(functools.partial(fused, cfg), out_shape=(jax.ShapeDtypeSt...  22.7 us
    unnamed x2, local copies, waits for them, and re-layouts  3.18 us

profile of v2, /device:TPU:0, one launch (start us, length us, event | category | flops | bytes accessed | tf_op | source)
XLA Modules:
  0.0 26.5 jit_solution(6174749697183413764)
XLA Ops:
  0.6 22.7 %transient_fstat.1 = (f32[512,256]{1,0:T(8,128)}, f32[16,32]{1,0:T(8,128)}) custom-call(s32[2,256]{1,0:T(2,128)} %bitcast.6, bf16[32,4,8192]{2,1,0:T(4,128)(2,1)} %spec_ref.1, f32[1,256]{1,0:T(1,128)} %bitcast.7, f32[4,512]{1,0:T(4,128)} %bitcast.5, s32[32]{0:T(128)} %starts_in.1, s32[32]{0:T(128)} %dur_in.1), custom_call_target="tpu_custom_call" | custom-call | tf_op jit(solution)/shard_map/transient_fstat/pallas_call | solution.py:312
  23.4 1.9 %copy.10 = f32[16,32,256]{2,1,0:T(8,128)} copy(f32[16,32,256]{2,1,0:T(8,128)} %bitcast.4) | data formatting | bytes 1048576
  25.3 1.3 %copy.11 = f32[16,32]{1,0:T(8,128)} copy(f32[16,32]{1,0:T(8,128)} %get-tuple-element.9) | data formatting | bytes 4096

commit v3 on v2

--- a/solution.py
+++ b/solution.py
@@ -24,9 +24,9 @@
 def fused(
     cfg,
     off_in, spec_ref, frac_in, ant_in, starts_in, dur_in,
-    fstat_out, loud_ref,
-    off_ref, frac_ref, ant_ref, starts_ref, dur_ref, fstat_ref, small_sem, fstat_sem,
-    xbuf, xf, off_send, off_recv, wsend, wall, mask, lsend, lrecv,
+    fstat_ref, loud_ref,
+    off_ref, frac_ref, ant_ref, starts_ref, dur_ref, small_sem,
+    xbuf, xf, off_send, off_recv, places, wsend, wall, mask, lsend, lrecv,
     spec_sem, osend_sem, orecv_sem, wsend_sem, wrecv_sem, lsend_sem, lrecv_sem,
 ):
     bands, times, rows, nb, chunks, nsft, grid, my_rows = cfg
@@ -62,7 +62,7 @@
     small[0].wait()
     off_send[...] = jnp.zeros_like(off_send)
     for t in range(bands):
-        off_send[t, 0:nb, 0:rows] = off_ref[:, t * rows:(t + 1) * rows]
+        off_send[t, :, 0:rows] = off_ref[:, t * rows:(t + 1) * rows]
     off_recv[t_me] = off_send[t_me]
     small[1].wait()
     small[2].wait()
@@ -138,18 +138,25 @@
             device_id={"tmpl": t, "tm": m}, device_id_type=MESH,
         )
 
+    def off_arrive(k, carry):
+        off_arrival(k).wait_recv()
+        return carry
+
+    lax.fori_loop(1, bands, off_arrive, 0)
+    columns = jnp.transpose(
+        jnp.concatenate([off_recv[t] for t in range(bands)], axis=0)
+    )[0:rows, :]
+    for t in range(bands):
+        place = jnp.zeros((rows, LANES), jnp.int32)
+        for b in range(nb):
+            at = t * nb + b
+            place = jnp.where(lane_b == b, columns[:, at:at + 1], place)
+        places[t] = place + lane_m
+
     def pick(k, carry):
         t = lax.rem(t_me + k, bands)
 
-        @pl.when(k < bands)
-        def _():
-            off_arrival(k).wait_recv()
-
-        columns = jnp.transpose(off_recv[t])[0:rows, :]
-        place = jnp.zeros((rows, LANES), jnp.int32)
-        for b in range(nb):
-            place = jnp.where(lane_b == b, columns[:, b:b + 1], place)
-        place = place + lane_m
+        place = places[t]
         chunk = place // LANES
         spot = place % LANES
         picked = [jnp.zeros((rows, LANES), F32) for _ in range(4)]
@@ -216,10 +223,6 @@
 
     step = 128
 
-    def fstat_copy(r):
-        part = pl.ds(r * step, step)
-        return pltpu.make_async_copy(fstat_ref.at[part], fstat_out.at[part], fstat_sem.at[r])
-
     for r in range(my_rows * grid // step):
         at = slice(r * step, (r + 1) * step)
         total = jnp.dot(mask[at, :], everything, preferred_element_type=F32)
@@ -232,7 +235,6 @@
         top = wb * (ra * ra + ia * ia) + wa * (rb * rb + ib * ib) - (2.0 * wc) * (ra * rb + ia * ib)
         stat = top * inverse
         fstat_ref[at, :] = stat
-        fstat_copy(r).start()
         best = stat[:, 0:LANES]
         for q in range(1, width // LANES):
             best = jnp.maximum(best, stat[:, q * LANES:(q + 1) * LANES])
@@ -290,8 +292,6 @@
         return carry
 
     lax.fori_loop(1, bands, loud_done, 0)
-    for r in range(my_rows * grid // step):
-        fstat_copy(r).wait()
 
 
 def body(spectra, offsets, fractions, antenna, starts, durations):
@@ -308,7 +308,7 @@
     cells = my_rows * grid
     cfg = (bands, times, rows, nb, chunks, nsft, grid, my_rows)
     vmem = pl.BlockSpec(memory_space=pltpu.VMEM)
-    anywhere = pl.BlockSpec(memory_space=pl.ANY)
+    anywhere = pl.BlockSpec(memory_space=pltpu.HBM)
     fstat, loudest = pl.pallas_call(
         functools.partial(fused, cfg),
         out_shape=(
@@ -316,20 +316,19 @@
             jax.ShapeDtypeStruct((my_rows, grid), F32),
         ),
         in_specs=[anywhere] * 6,
-        out_specs=(anywhere, vmem),
+        out_specs=(vmem, vmem),
         scratch_shapes=[
             pltpu.VMEM((nb, offsets.shape[0]), jnp.int32),
             pltpu.VMEM((1, width), F32),
             pltpu.VMEM((4, nsft), F32),
             pltpu.SMEM((grid,), jnp.int32),
             pltpu.SMEM((grid,), jnp.int32),
-            pltpu.VMEM((cells, width), F32),
             pltpu.SemaphoreType.DMA((5,)),
-            pltpu.SemaphoreType.DMA((cells // 128,)),
             pltpu.VMEM((rows, 4, bins), BF16),
             pltpu.VMEM((bins // LANES, rows * 4, LANES), F32),
-            pltpu.VMEM((bands, 8, LANES), jnp.int32),
-            pltpu.VMEM((bands, 8, LANES), jnp.int32),
+            pltpu.VMEM((bands, nb, LANES), jnp.int32),
+            pltpu.VMEM((bands, nb, LANES), jnp.int32),
+            pltpu.VMEM((bands, rows, LANES), jnp.int32),
             pltpu.VMEM((bands, rows, LANES), BF16),
             pltpu.VMEM((group, rows, LANES), BF16),
             pltpu.VMEM((cells, nsft), BF16),
@@ -344,10 +343,13 @@
             pltpu.SemaphoreType.DMA((bands,)),
         ],
         compiler_params=pltpu.CompilerParams(
-            collective_id=0, has_side_effects=True, vmem_limit_bytes=60 * 1024 * 1024
+            collective_id=0, has_side_effects=True, vmem_limit_bytes=32 * 1024 * 1024
         ),
         name="transient_fstat",
-    )(offsets.T, spectra, fractions.reshape(1, width), antenna.T, starts, durations)
+    )(*[
+        pltpu.with_memory_space_constraint(x, pltpu.HBM)
+        for x in (offsets.T, spectra, fractions.reshape(1, width), antenna.T, starts, durations)
+    ])
     return fstat.reshape(my_rows, grid, width), loudest
 
 

time: 26.8 us -> 24.1 us (0.90)
  local copies, waits for them, and re-layouts: 3.18 us -> 1.39 us
  Pallas kernels: 22.7 us -> 21.9 us
    unnamed x2, local copies, waits for them, and re-layouts: 3.18 us -> 1.39 us
    pallas_call x1, Pallas kernels: 22.7 us -> 21.9 us  [body(): pl.pallas_call(functools.partial(fused, cfg), out_shape=(jax.ShapeDtypeSt...]
where the time goes in v3:
time: 24.1 us; the launch traced here: 23.9 us
  Pallas kernels  21.9 us (91%)
  local copies, waits for them, and re-layouts  1.39 us (6%)
  between operations  0.64 us (3%)
    pallas_call x1, Pallas kernels, body(): pl.pallas_call(functools.partial(fused, cfg), out_shape=(jax.ShapeDtypeSt...  21.9 us
    unnamed x2, local copies, waits for them, and re-layouts  1.39 us

profile of v3, /device:TPU:0, one launch (start us, length us, event | category | flops | bytes accessed | tf_op | source)
XLA Modules:
  0.0 23.9 jit_solution(6207261037612689319)
XLA Ops:
  0.6 21.9 %transient_fstat.1 = (f32[512,256]{1,0:T(8,128)S(1)}, f32[16,32]{1,0:T(8,128)S(1)}) custom-call(s32[2,256]{1,0:T(2,128)} %bitcast.6, bf16[32,4,8192]{2,1,0:T(4,128)(2,1)} %spec_ref.1, f32[1,256]{1,0:T(1,128)} %bitcast.7, f32[4,512]{1,0:T(4,128)} %bitcast.5, s32[32]{0:T(128)} %starts_in.1, s32[32]{0:T(128)} %dur_in.1), custom_call_target="tpu_custom_call" | custom-call | tf_op jit(solution)/shard_map/transient_fstat/pallas_call | solution.py:312
  22.6 0.8 %copy.10 = f32[16,32,256]{2,1,0:T(8,128)} copy(f32[16,32,256]{2,1,0:T(8,128)S(1)} %bitcast.4) | data formatting | bytes 1048576
  23.3 0.6 %copy.11 = f32[16,32]{1,0:T(8,128)} copy(f32[16,32]{1,0:T(8,128)S(1)} %get-tuple-element.9) | data formatting | bytes 4096

commit v4 on v3

--- a/solution.py
+++ b/solution.py
@@ -147,25 +147,27 @@
         jnp.concatenate([off_recv[t] for t in range(bands)], axis=0)
     )[0:rows, :]
     for t in range(bands):
-        place = jnp.zeros((rows, LANES), jnp.int32)
         for b in range(nb):
             at = t * nb + b
-            place = jnp.where(lane_b == b, columns[:, at:at + 1], place)
-        places[t] = place + lane_m
+            places[at] = jnp.broadcast_to(columns[:, at:at + 1], (rows, LANES))
 
     def pick(k, carry):
         t = lax.rem(t_me + k, bands)
 
-        place = places[t]
-        chunk = place // LANES
-        spot = place % LANES
-        picked = [jnp.zeros((rows, LANES), F32) for _ in range(4)]
-        for ch in range(chunks):
-            here = chunk == ch
+        picked = [None] * 4
+        for b in range(nb):
+            begin_b = places[t * nb + b]
+            wanted = begin_b // LANES + (lane < begin_b % LANES).astype(jnp.int32)
+            spot = (begin_b + lane_m) % LANES
+            source = [jnp.zeros((rows, LANES), F32) for _ in range(4)]
+            for ch in range(chunks):
+                here = wanted == ch
+                for c in range(4):
+                    piece = xf[t * chunks + ch, pl.ds(c, rows, stride=4), :]
+                    source[c] = jnp.where(here, piece, source[c])
             for c in range(4):
-                piece = xf[t * chunks + ch, pl.ds(c, rows, stride=4), :]
-                got = jnp.take_along_axis(piece, spot, axis=1, mode="promise_in_bounds")
-                picked[c] = jnp.where(here, got, picked[c])
+                got = jnp.take_along_axis(source[c], spot, axis=1, mode="promise_in_bounds")
+                picked[c] = got if b == 0 else jnp.where(lane_b == b, got, picked[c])
         one = jnp.where(even, picked[0], picked[1])
         two = jnp.where(even, picked[2], picked[3])
         wsend[t] = (coef_p * one + coef_q * two).astype(BF16)
@@ -328,7 +330,7 @@
             pltpu.VMEM((bins // LANES, rows * 4, LANES), F32),
             pltpu.VMEM((bands, nb, LANES), jnp.int32),
             pltpu.VMEM((bands, nb, LANES), jnp.int32),
-            pltpu.VMEM((bands, rows, LANES), jnp.int32),
+            pltpu.VMEM((bands * nb, rows, LANES), jnp.int32),
             pltpu.VMEM((bands, rows, LANES), BF16),
             pltpu.VMEM((group, rows, LANES), BF16),
             pltpu.VMEM((cells, nsft), BF16),

time: 24.1 us -> 22.6 us (0.938)
  Pallas kernels: 21.9 us -> 20.4 us
    pallas_call x1, Pallas kernels: 21.9 us -> 20.4 us  [body(): pl.pallas_call(functools.partial(fused, cfg), out_shape=(jax.ShapeDtypeSt...]
where the time goes in v4:
time: 22.6 us; the launch traced here: 22.4 us
  Pallas kernels  20.4 us (90%)
  local copies, waits for them, and re-layouts  1.39 us (6%)
  between operations  0.64 us (3%)
    pallas_call x1, Pallas kernels, body(): pl.pallas_call(functools.partial(fused, cfg), out_shape=(jax.ShapeDtypeSt...  20.4 us
    unnamed x2, local copies, waits for them, and re-layouts  1.39 us

profile of v4, /device:TPU:0, one launch (start us, length us, event | category | flops | bytes accessed | tf_op | source)
XLA Modules:
  0.0 22.4 jit_solution(9563519399996311950)
XLA Ops:
  0.6 20.4 %transient_fstat.1 = (f32[512,256]{1,0:T(8,128)S(1)}, f32[16,32]{1,0:T(8,128)S(1)}) custom-call(s32[2,256]{1,0:T(2,128)} %bitcast.6, bf16[32,4,8192]{2,1,0:T(4,128)(2,1)} %spec_ref.1, f32[1,256]{1,0:T(1,128)} %bitcast.7, f32[4,512]{1,0:T(4,128)} %bitcast.5, s32[32]{0:T(128)} %starts_in.1, s32[32]{0:T(128)} %dur_in.1), custom_call_target="tpu_custom_call" | custom-call | tf_op jit(solution)/shard_map/transient_fstat/pallas_call | solution.py:314
  21.0 0.8 %copy.10 = f32[16,32,256]{2,1,0:T(8,128)} copy(f32[16,32,256]{2,1,0:T(8,128)S(1)} %bitcast.4) | data formatting | bytes 1048576
  21.8 0.6 %copy.11 = f32[16,32]{1,0:T(8,128)} copy(f32[16,32]{1,0:T(8,128)S(1)} %get-tuple-element.9) | data formatting | bytes 4096

commit v5 on v4

--- a/solution.py
+++ b/solution.py
@@ -177,7 +177,7 @@
                 window_copy(t, m).start()
         return carry
 
-    lax.fori_loop(1, bands + 1, pick, 0)
+    lax.fori_loop(1, bands + 1, pick, 0, unroll=2)
     wall[me] = wsend[t_me]
 
     ant = ant_ref[...]
@@ -223,7 +223,7 @@
     lax.fori_loop(1, group, arrive, 0)
     everything = wall[...].reshape(nsft, LANES)
 
-    step = 128
+    step = 256
 
     for r in range(my_rows * grid // step):
         at = slice(r * step, (r + 1) * step)

time: 22.6 us -> 22.4 us (level)
  no operation moved by 1% of the time
where the time goes in v5:
time: 22.4 us; the launch traced here: 22.3 us
  Pallas kernels  20.2 us (90%)
  local copies, waits for them, and re-layouts  1.39 us (6%)
  between operations  0.64 us (3%)
    pallas_call x1, Pallas kernels, body(): pl.pallas_call(functools.partial(fused, cfg), out_shape=(jax.ShapeDtypeSt...  20.2 us
    unnamed x2, local copies, waits for them, and re-layouts  1.39 us

profile of v5, /device:TPU:0, one launch (start us, length us, event | category | flops | bytes accessed | tf_op | source)
XLA Modules:
  0.0 22.3 jit_solution(12204287645815079758)
XLA Ops:
  0.6 20.2 %transient_fstat.1 = (f32[512,256]{1,0:T(8,128)S(1)}, f32[16,32]{1,0:T(8,128)S(1)}) custom-call(s32[2,256]{1,0:T(2,128)} %bitcast.6, bf16[32,4,8192]{2,1,0:T(4,128)(2,1)} %spec_ref.1, f32[1,256]{1,0:T(1,128)} %bitcast.7, f32[4,512]{1,0:T(4,128)} %bitcast.5, s32[32]{0:T(128)} %starts_in.1, s32[32]{0:T(128)} %dur_in.1), custom_call_target="tpu_custom_call" | custom-call | tf_op jit(solution)/shard_map/transient_fstat/pallas_call | solution.py:314
  20.9 0.8 %copy.10 = f32[16,32,256]{2,1,0:T(8,128)} copy(f32[16,32,256]{2,1,0:T(8,128)S(1)} %bitcast.4) | data formatting | bytes 1048576
  21.7 0.6 %copy.11 = f32[16,32]{1,0:T(8,128)} copy(f32[16,32]{1,0:T(8,128)S(1)} %get-tuple-element.9) | data formatting | bytes 4096
